TPU v7x, 256 devices: a whole 4x4x8 slice. The times are simulated.
256 devices in a mesh: dp: 4 (over y), expert: 16 (over z, core), ffn: 4 (over x).
Axes of the slice: x: 4, y: 4, z: 8, core: 2. Of those that a mesh axis runs over, the one named last changes fastest.
Arguments:
- tokens: bfloat16 [8192, 7168], P(('dp', 'expert'), 'ffn'), may hold values from -6 to 6
- grad_out: bfloat16 [8192, 7168], P(('dp', 'expert'), 'ffn'), may hold values from -3 to 3
- route_ids: int32 [8192, 2], P(('dp', 'expert')), may hold values from 0 to 15, all different within a row; in each aligned block of 128 rows (0 to 127, 128 to 255, ...) at most 20 rows name the same one
- combine: float32 [8192, 2], P(('dp', 'expert')), may hold values from 0.2 to 1
- gate_weight: bfloat16 [16, 7168, 1024], P('expert', 'dp', 'ffn'), may hold values from -0.0625 to 0.0625
- up_weight: bfloat16 [16, 7168, 1024], P('expert', 'dp', 'ffn'), may hold values from -0.0625 to 0.0625
- down_weight: bfloat16 [16, 1024, 7168], P('expert', 'ffn', 'dp'), may hold values from -0.1875 to 0.1875
Outputs:
- grad_tokens: bfloat16 [8192, 7168], P(('dp', 'expert'), 'ffn')
- grad_gate: float32 [16, 7168, 1024], P('expert', 'dp', 'ffn')
- grad_up: float32 [16, 7168, 1024], P('expert', 'dp', 'ffn')
- grad_down: float32 [16, 1024, 7168], P('expert', 'ffn', 'dp')
Inputs may be any that keep to these rules, and one draw needn't show every extreme that they name: `route_ids`: each row names 2 different experts; every expert is named by some row. In each aligned block of 128 rows (the rows of one device) no expert is named by more than 20 rows, a bound that some block reaches.
All inputs are finite; a program needn't handle non-finite values.
Results may differ from a plain program's by a relative error of at most 0.019.
Values may be sent and summed in bfloat16 or wider, within the bound.
No kernel may reach another device: no remote copies, remote signals or barrier semaphores. Data moves between devices by JAX's collectives and lax.ppermute only.
A program may use at most 128 MiB of HBM per device.

v0:
```python
import jax
import jax.numpy as jnp
from jax import lax
from jax.sharding import PartitionSpec as P


def activations(gate, up, grad_hidden):
    sig = jax.nn.sigmoid(gate)
    hidden = (gate * sig * up).astype(jnp.bfloat16)
    grad_up_act = (grad_hidden * gate * sig).astype(jnp.bfloat16)
    grad_gate_act = (grad_hidden * up * sig * (1.0 + gate * (1.0 - sig))).astype(jnp.bfloat16)
    return (hidden, grad_up_act, grad_gate_act)


def per_device(tokens, grad_out, route_ids, combine, gate_weight, up_weight, down_weight):
    tok_rows = tokens.shape[0]
    top = route_ids.shape[1]
    groups = lax.axis_size("expert")
    experts = gate_weight.shape[0] * groups
    capacity = min(tok_rows, (5 * top * tok_rows + 4 * experts - 1) // (4 * experts))
    slot_count = tok_rows * top
    expert_of = route_ids.reshape(slot_count)
    onehot = (expert_of[:, None] == jnp.arange(experts, dtype=jnp.int32)[None, :]).astype(jnp.int32)
    earlier = jnp.cumsum(onehot, axis=0) - onehot
    position = jnp.sum(earlier * onehot, axis=1)
    target = expert_of * capacity + position
    placing = (jnp.arange(experts * capacity, dtype=jnp.int32)[:, None] == target[None, :]).astype(
        jnp.bfloat16
    )
    placing_tok = jnp.sum(placing.reshape(experts * capacity, tok_rows, top), axis=2)
    scaled = (combine[:, :, None] * grad_out[:, None, :].astype(jnp.float32)).astype(jnp.bfloat16)
    scaled = scaled.reshape(slot_count, grad_out.shape[1])

    def pack(matrix, rows):
        packed = jnp.dot(matrix, rows, preferred_element_type=jnp.float32).astype(jnp.bfloat16)
        return packed.reshape(groups, capacity, rows.shape[1])

    full_tok, full_z = (
        lax.all_gather(tokens, "ffn", axis=1, tiled=True),
        lax.all_gather(scaled, "ffn", axis=1, tiled=True),
    )
    recv_x, recv_z = (
        lax.all_to_all(
            pack(placing_tok, full_tok), "expert", split_axis=0, concat_axis=0, tiled=True
        ),
        lax.all_to_all(pack(placing, full_z), "expert", split_axis=0, concat_axis=0, tiled=True),
    )
    width = recv_x.shape[2]
    row_count = groups * capacity
    x_rows = recv_x.reshape(row_count, width)
    z_rows = recv_z.reshape(row_count, width)
    over_rows = (((0,), (0,)), ((), ()))
    over_units = (((1,), (1,)), ((), ()))
    gathered_w = (
        lax.all_gather(gate_weight, "dp", axis=1, tiled=True),
        lax.all_gather(up_weight, "dp", axis=1, tiled=True),
        lax.all_gather(down_weight, "dp", axis=2, tiled=True),
    )
    w_gate = gathered_w[0][0]
    w_up = gathered_w[1][0]
    w_down = gathered_w[2][0]
    gate = jnp.dot(x_rows, w_gate, preferred_element_type=jnp.float32)
    up = jnp.dot(x_rows, w_up, preferred_element_type=jnp.float32)
    grad_hidden = lax.dot_general(z_rows, w_down, over_units, preferred_element_type=jnp.float32)
    hidden, grad_up_act, grad_gate_act = activations(gate, up, grad_hidden)
    part_gate = lax.dot_general(
        x_rows, grad_gate_act, over_rows, preferred_element_type=jnp.float32
    )
    part_up = lax.dot_general(x_rows, grad_up_act, over_rows, preferred_element_type=jnp.float32)
    part_down = lax.dot_general(hidden, z_rows, over_rows, preferred_element_type=jnp.float32)
    grad_gate, grad_up, grad_down = (
        lax.psum_scatter(
            part_gate[None].astype(jnp.bfloat16), "dp", scatter_dimension=1, tiled=True
        ).astype(jnp.float32),
        lax.psum_scatter(
            part_up[None].astype(jnp.bfloat16), "dp", scatter_dimension=1, tiled=True
        ).astype(jnp.float32),
        lax.psum_scatter(
            part_down[None].astype(jnp.bfloat16), "dp", scatter_dimension=2, tiled=True
        ).astype(jnp.float32),
    )
    slot_partial = lax.dot_general(
        grad_gate_act, w_gate, over_units, preferred_element_type=jnp.float32
    )
    slot_partial = slot_partial + lax.dot_general(
        grad_up_act, w_up, over_units, preferred_element_type=jnp.float32
    )
    summed = lax.psum_scatter(
        slot_partial.astype(jnp.bfloat16), "ffn", scatter_dimension=1, tiled=True
    )
    piece = summed.shape[1]
    returned = lax.all_to_all(
        summed.reshape(groups, capacity, piece), "expert", split_axis=0, concat_axis=0, tiled=True
    )
    slot_grad = returned.reshape(experts * capacity, piece)
    per_slot = lax.dot_general(placing, slot_grad, over_rows, preferred_element_type=jnp.float32)
    grad_tokens = jnp.sum(per_slot.reshape(tok_rows, top, slot_grad.shape[1]), axis=1).astype(
        jnp.bfloat16
    )
    return (grad_tokens, grad_gate, grad_up, grad_down)


def solution(mesh):
    return jax.shard_map(
        per_device,
        mesh=mesh,
        in_specs=(
            P(("dp", "expert"), "ffn"),
            P(("dp", "expert"), "ffn"),
            P(("dp", "expert"), None),
            P(("dp", "expert"), None),
            P("expert", "dp", "ffn"),
            P("expert", "dp", "ffn"),
            P("expert", "ffn", "dp"),
        ),
        out_specs=(
            P(("dp", "expert"), "ffn"),
            P("expert", "dp", "ffn"),
            P("expert", "dp", "ffn"),
            P("expert", "ffn", "dp"),
        ),
        check_vma=False,
    )
```

profile of v0, /device:TPU:1, one launch (start us, length us, event | category | flops | bytes accessed | tf_op | source)
XLA Modules:
  0.0 535.1 jit_solution(14944798309835122971)
XLA Ops:
  16.9 27.7 %all-gather.10.cloned.1.call-done = bf16[128,7168]{1,0:T(8,128)(2,1)} async-done(((bf16[128,1792]{1,0:T(8,128)(2,1)}), bf16[128,7168]{1,0:T(8,128)(2,1)}) %all-gather.10.cloned.1.call-update) | async-done | bytes 1835024 | tf_op jit(solution)/shard_map/all_gather | solution.py:39
  44.6 4.9 convolution_convert_fusion
  49.5 7.3 %reshape.104 = bf16[16,20,7168]{2,1,0:T(8,128)(2,1)} reshape(bf16[320,7168]{1,0:T(8,128)(2,1)} %convolution_convert_fusion) | data formatting | bytes 9175040 | tf_op jit(solution)/shard_map/reshape | solution.py:36
  56.8 7.9 %all-to-all-start.1 = ((bf16[16,20,7168]{2,1,0:T(8,128)(2,1)}), bf16[16,20,7168]{2,1,0:T(8,128)(2,1)}, u32[]{:S(2)}, u32[]{:S(2)}) async-start(bf16[16,20,7168]{2,1,0:T(8,128)(2,1)} %reshape.104), calls=%async_computation.1 | async-start | bytes 11010048 | tf_op jit(solution)/shard_map/all_to_all | solution.py:43
  66.0 27.3 %all-gather.6.cloned.1.call-done = bf16[256,7168]{1,0:T(8,128)(2,1)} async-done(((bf16[256,1792]{1,0:T(8,128)(2,1)}), bf16[256,7168]{1,0:T(8,128)(2,1)}) %all-gather.6.cloned.1.call-update) | async-done | bytes 3670032 | tf_op jit(solution)/shard_map/all_gather | solution.py:40
  93.4 5.5 %convolution_convert_fusion.1 = bf16[320,7168]{1,0:T(8,128)(2,1)} fusion(bf16[256,7168]{1,0:T(8,128)(2,1)} %all-gather.6.cloned.1.call-done, s32[256]{0:T(256)S(1)} %multiply_add_fusion.1), kind=kOutput, calls=%fused_computation.2 | convolution fusion | flops 1176780800 | bytes 8258560 | tf_op jit(solution)/shard_map/dot_general | solution.py:35
  98.8 7.3 %reshape.102 = bf16[16,20,7168]{2,1,0:T(8,128)(2,1)} reshape(bf16[320,7168]{1,0:T(8,128)(2,1)} %convolution_convert_fusion.1) | data formatting | bytes 9175040 | tf_op jit(solution)/shard_map/reshape | solution.py:36
  106.1 80.2 %all-to-all-done.1 = bf16[16,20,7168]{2,1,0:T(8,128)(2,1)} async-done(((bf16[16,20,7168]{2,1,0:T(8,128)(2,1)}), bf16[16,20,7168]{2,1,0:T(8,128)(2,1)}, u32[]{:S(2)}, u32[]{:S(2)}) %all-to-all-start.1) | async-done | bytes 4587552 | tf_op jit(solution)/shard_map/all_to_all | solution.py:43
  186.3 5.5 %all-to-all-start = ((bf16[16,20,7168]{2,1,0:T(8,128)(2,1)}), bf16[16,20,7168]{2,1,0:T(8,128)(2,1)}, u32[]{:S(2)}, u32[]{:S(2)}) async-start(bf16[16,20,7168]{2,1,0:T(8,128)(2,1)} %reshape.102), calls=%async_computation | async-start | bytes 11010048 | tf_op jit(solution)/shard_map/all_to_all | solution.py:46
  192.6 7.3 %reshape.105 = bf16[320,7168]{1,0:T(8,128)(2,1)} reshape(bf16[16,20,7168]{2,1,0:T(8,128)(2,1)} %all-to-all-done.1) | data formatting | bytes 9175040 | tf_op jit(solution)/shard_map/reshape | solution.py:50
  200.0 4.8 fusion.6
  204.8 5.4 %fusion.9 = f32[320,256]{1,0:T(8,128)S(1)} fusion(bf16[320,7168]{1,0:T(8,128)(2,1)} %reshape.105, bf16[1,7168,256]{2,1,0:T(8,128)(2,1)} %all-gather.12.cloned.1.call-done), kind=kOutput, calls=%fused_computation.15 | convolution fusion | flops 1174405120 | bytes 8585216 | tf_op jit(solution)/shard_map/dot_general | solution.py:63
  210.2 103.2 %all-to-all-done = bf16[16,20,7168]{2,1,0:T(8,128)(2,1)} async-done(((bf16[16,20,7168]{2,1,0:T(8,128)(2,1)}), bf16[16,20,7168]{2,1,0:T(8,128)(2,1)}, u32[]{:S(2)}, u32[]{:S(2)}) %all-to-all-start) | async-done | bytes 4587552 | tf_op jit(solution)/shard_map/all_to_all | solution.py:46
  313.4 7.3 %reshape.103 = bf16[320,7168]{1,0:T(8,128)(2,1)} reshape(bf16[16,20,7168]{2,1,0:T(8,128)(2,1)} %all-to-all-done) | data formatting | bytes 9175040 | tf_op jit(solution)/shard_map/reshape | solution.py:51
  320.8 5.0 multiply_convert_fusion.2
  327.8 3.6 fusion
  331.4 6.2 %fusion.3 = bf16[1,256,7168]{2,1,0:T(8,128)(2,1)} fusion(bf16[320,7168]{1,0:T(8,128)(2,1)} %reshape.103, f32[320,256]{1,0:T(8,128)S(1)} %fusion.9, f32[320,256]{1,0:T(8,128)S(1)} %fusion.6), kind=kOutput, calls=%fused_computation.9 | convolution fusion | flops 1176731648 | bytes 8912896 | tf_op jit(solution)/shard_map/dot_general | solution.py:70
  337.7 6.3 %fusion.2 = bf16[1,7168,256]{2,1,0:T(8,128)(2,1)} fusion(bf16[320,7168]{1,0:T(8,128)(2,1)} %reshape.105, bf16[320,256]{1,0:T(8,128)(2,1)S(1)} %get-tuple-element.4), kind=kOutput, calls=%fused_computation.8 | convolution fusion | flops 1176240128 | bytes 8421376 | tf_op jit(solution)/shard_map/dot_general | solution.py:69
  344.3 6.3 %fusion.1 = bf16[1,7168,256]{2,1,0:T(8,128)(2,1)} fusion(bf16[320,7168]{1,0:T(8,128)(2,1)} %reshape.105, bf16[320,256]{1,0:T(8,128)(2,1)S(1)} %get-tuple-element.5), kind=kOutput, calls=%fused_computation.7 | convolution fusion | flops 1176240128 | bytes 8421376 | tf_op jit(solution)/shard_map/dot_general | solution.py:66
  350.6 31.3 %reduce-scatter.5.cloned.1.call-done = bf16[320,1792]{1,0:T(8,128)(2,1)} async-done(((bf16[320,7168]{1,0:T(8,128)(2,1)}), bf16[320,1792]{1,0:T(8,128)(2,1)}) %reduce-scatter.5.cloned.1.call-update) | async-done | bytes 1146896 | tf_op jit(solution)/shard_map/reduce_scatter | solution.py:88
  384.2 7.8 %all-to-all-start.2 = ((bf16[16,20,1792]{2,1,0:T(8,128)(2,1)}), bf16[16,20,1792]{2,1,0:T(8,128)(2,1)S(1)}, u32[]{:S(2)}, u32[]{:S(2)}) async-start(bf16[16,20,1792]{2,1,0:T(8,128)(2,1)} %reshape.106), calls=%async_computation.3 | async-start | bytes 2752512 | tf_op jit(solution)/shard_map/all_to_all | solution.py:92
  392.2 37.2 %reduce-scatter.11.cloned.1.call-done = bf16[1,256,1792]{2,1,0:T(8,128)(2,1)} async-done(((bf16[1,256,7168]{2,1,0:T(8,128)(2,1)}), bf16[1,256,1792]{2,1,0:T(8,128)(2,1)}) %reduce-scatter.11.cloned.1.call-update) | async-done | bytes 917520 | tf_op jit(solution)/shard_map/reduce_scatter | solution.py:78
  431.9 44.9 %reduce-scatter.9.cloned.1.call-done = bf16[1,1792,256]{2,1,0:T(8,128)(2,1)} async-done(((bf16[1,7168,256]{2,1,0:T(8,128)(2,1)}), bf16[1,1792,256]{2,1,0:T(8,128)(2,1)}) %reduce-scatter.9.cloned.1.call-update) | async-done | bytes 917520 | tf_op jit(solution)/shard_map/reduce_scatter | solution.py:75
  479.4 44.9 %reduce-scatter.7.cloned.1.call-done = bf16[1,1792,256]{2,1,0:T(8,128)(2,1)} async-done(((bf16[1,7168,256]{2,1,0:T(8,128)(2,1)}), bf16[1,1792,256]{2,1,0:T(8,128)(2,1)}) %reduce-scatter.7.cloned.1.call-update) | async-done | bytes 917520 | tf_op jit(solution)/shard_map/reduce_scatter | solution.py:72
  (56 shorter events, 26.0 us)
Async XLA Ops:
  7.2 37.4 %all-gather.10.cloned.1.call-start = ((), (), s32[]{:S(2)}) async-start(), calls=%async_computation.9 | async-start | bytes 2293760 | tf_op jit(solution)/shard_map/all_gather | solution.py:39
  7.9 85.5 %all-gather.6.cloned.1.call-start = ((), (), s32[]{:S(2)}) async-start(), calls=%async_computation.7 | async-start | bytes 4587520 | tf_op jit(solution)/shard_map/all_gather | solution.py:40
  11.6 3.7 copy-start.2
  56.8 129.5 %all-to-all-start.1 = ((bf16[16,20,7168]{2,1,0:T(8,128)(2,1)}), bf16[16,20,7168]{2,1,0:T(8,128)(2,1)}, u32[]{:S(2)}, u32[]{:S(2)}) async-start(bf16[16,20,7168]{2,1,0:T(8,128)(2,1)} %reshape.104), calls=%async_computation.1 | async-start | bytes 11010048 | tf_op jit(solution)/shard_map/all_to_all | solution.py:43
  64.7 135.3 %all-gather.14.cloned.1.call-start = ((), (), s32[]{:S(2)}) async-start(), calls=%async_computation.11 | async-start | bytes 4587520 | tf_op jit(solution)/shard_map/all_gather | solution.py:55
  65.4 139.3 %all-gather.12.cloned.1.call-start = ((), (), s32[]{:S(2)}) async-start(), calls=%async_computation.10 | async-start | bytes 4587520 | tf_op jit(solution)/shard_map/all_gather | solution.py:56
  186.3 127.1 %all-to-all-start = ((bf16[16,20,7168]{2,1,0:T(8,128)(2,1)}), bf16[16,20,7168]{2,1,0:T(8,128)(2,1)}, u32[]{:S(2)}, u32[]{:S(2)}) async-start(bf16[16,20,7168]{2,1,0:T(8,128)(2,1)} %reshape.102), calls=%async_computation | async-start | bytes 11010048 | tf_op jit(solution)/shard_map/all_to_all | solution.py:46
  191.8 128.9 %all-gather.8.cloned.1.call-start = ((), (), s32[]{:S(2)}) async-start(), calls=%async_computation.8 | async-start | bytes 4587520 | tf_op jit(solution)/shard_map/all_gather | solution.py:57
  192.4 189.5 %reduce-scatter.5.cloned.1.call-start = ((), (), s32[]{:S(2)}) async-start(), calls=%async_computation.12 | async-start | bytes 5734400 | tf_op jit(solution)/shard_map/reduce_scatter | solution.py:88
  320.8 5.0 copy-start
  325.7 2.0 copy-start.1
  331.4 98.0 %reduce-scatter.11.cloned.1.call-start = ((), (), s32[]{:S(2)}) async-start(), calls=%async_computation.15 | async-start | bytes 4587520 | tf_op jit(solution)/shard_map/reduce_scatter | solution.py:78
  337.7 139.1 %reduce-scatter.9.cloned.1.call-start = ((), (), s32[]{:S(2)}) async-start(), calls=%async_computation.14 | async-start | bytes 4587520 | tf_op jit(solution)/shard_map/reduce_scatter | solution.py:75
  344.0 180.3 %reduce-scatter.7.cloned.1.call-start = ((), (), s32[]{:S(2)}) async-start(), calls=%async_computation.13 | async-start | bytes 4587520 | tf_op jit(solution)/shard_map/reduce_scatter | solution.py:72
  384.2 142.7 %all-to-all-start.2 = ((bf16[16,20,1792]{2,1,0:T(8,128)(2,1)}), bf16[16,20,1792]{2,1,0:T(8,128)(2,1)S(1)}, u32[]{:S(2)}, u32[]{:S(2)}) async-start(bf16[16,20,1792]{2,1,0:T(8,128)(2,1)} %reshape.106), calls=%async_computation.3 | async-start | bytes 2752512 | tf_op jit(solution)/shard_map/all_to_all | solution.py:92
Sparse Core Ops, SparseCore 0:
  9.8 34.7 all-gather.9
  47.0 46.3 all-gather.5
  95.2 46.7 all-gather.13
  143.6 46.6 all-gather.11
  194.1 45.7 all-gather.7
  331.5 50.3 reduce-scatter.4
  384.4 44.8 reduce-scatter.10
  431.9 44.8 reduce-scatter.8
  479.4 44.8 reduce-scatter.6
where the time goes:
time: 536 us; the launch traced here: 535 us
  waiting for transfers between devices  399 us (74%)
  matrix products  50.7 us (9%)
  local copies, waits for them, and re-layouts  39.6 us (7%)
  starting transfers between devices  21.9 us (4%)
  between operations  14 us (3%)
  other arithmetic  9.62 us (2%)
    all_to_all x1, waiting for transfers between devices, per_device(): lax.all_to_all(pack(placing, full_z), 'expert', split_axis=0, concat_axis...  103 us
    all_to_all x1, waiting for transfers between devices, per_device(): lax.all_to_all(pack(placing_tok, full_tok), 'expert', split_axis=0, conca...  80.2 us
    reduce_scatter x1, waiting for transfers between devices, per_device(): lax.psum_scatter(part_up[None].astype(jnp.bfloat16), 'dp', scatter_dimens...  44.9 us
    reduce_scatter x1, waiting for transfers between devices, per_device(): lax.psum_scatter(part_gate[None].astype(jnp.bfloat16), 'dp', scatter_dime...  44.9 us
    reduce_scatter x1, waiting for transfers between devices, per_device(): lax.psum_scatter(part_down[None].astype(jnp.bfloat16), 'dp', scatter_dime...  37.2 us
    reduce_scatter x1, waiting for transfers between devices, per_device(): lax.psum_scatter(slot_partial.astype(jnp.bfloat16), 'ffn', scatter_dimens...  31.3 us
    all_gather x1, waiting for transfers between devices, per_device(): lax.all_gather(tokens, 'ffn', axis=1, tiled=True)  27.7 us
    all_gather x1, waiting for transfers between devices, per_device(): lax.all_gather(scaled, 'ffn', axis=1, tiled=True)  27.3 us
  transfers between devices with their start and end apart: 12, of which 8 were waited for; matrix products, arithmetic and copies ran while one was open for 16% of the time, Pallas kernels for 0%

commit v1 on v0

--- a/solution.py
+++ b/solution.py
@@ -37,7 +37,15 @@
 
     full_tok, full_z = (
         lax.all_gather(tokens, "ffn", axis=1, tiled=True),
-        lax.all_gather(scaled, "ffn", axis=1, tiled=True),
+        jnp.concatenate(
+            lax.all_to_all(
+                jnp.stack(lax.axis_size("ffn") * [scaled]),
+                axis_name="ffn",
+                split_axis=0,
+                concat_axis=0,
+            ),
+            1,
+        ),
     )
     recv_x, recv_z = (
         lax.all_to_all(

time: 536 us -> 572 us (1.067)
  waiting for transfers between devices: 399 us -> 423 us
  starting transfers between devices: 21.9 us -> 31 us
    all_to_all x1, waiting for transfers between devices: 80.2 us -> 108 us  [per_device(): lax.all_to_all(pack(placing_tok, full_tok), 'expert', split_axis=0, conca...]
    all_gather x1 -> x0, waiting for transfers between devices: 27.3 us -> none  [per_device(): lax.all_gather(scaled, 'ffn', axis=1, tiled=True)]
    all_to_all x1, waiting for transfers between devices: 103 us -> 113 us  [per_device(): lax.all_to_all(pack(placing, full_z), 'expert', split_axis=0, concat_axis...]
    all_gather x1, waiting for transfers between devices: 27.7 us -> 36 us  [per_device(): lax.all_gather(tokens, 'ffn', axis=1, tiled=True)]
    all_to_all x0 -> x1, waiting for transfers between devices: none -> 6.26 us  [per_device(): lax.all_to_all(jnp.stack(lax.axis_size('ffn') * [scaled]), axis_name='ffn...]
where the time goes in v1:
time: 572 us; the launch traced here: 571 us
  waiting for transfers between devices  423 us (74%)
  matrix products  50.2 us (9%)
  local copies, waits for them, and re-layouts  42.2 us (7%)
  starting transfers between devices  31 us (5%)
  between operations  15.6 us (3%)
  other arithmetic  8.69 us (2%)
    all_to_all x1, waiting for transfers between devices, per_device(): lax.all_to_all(pack(placing, full_z), 'expert', split_axis=0, concat_axis...  113 us
    all_to_all x1, waiting for transfers between devices, per_device(): lax.all_to_all(pack(placing_tok, full_tok), 'expert', split_axis=0, conca...  108 us
    reduce_scatter x1, waiting for transfers between devices, per_device(): lax.psum_scatter(part_up[None].astype(jnp.bfloat16), 'dp', scatter_dimens...  44.8 us
    reduce_scatter x1, waiting for transfers between devices, per_device(): lax.psum_scatter(part_gate[None].astype(jnp.bfloat16), 'dp', scatter_dime...  44.8 us
    reduce_scatter x1, waiting for transfers between devices, per_device(): lax.psum_scatter(part_down[None].astype(jnp.bfloat16), 'dp', scatter_dime...  37.2 us
    all_gather x1, waiting for transfers between devices, per_device(): lax.all_gather(tokens, 'ffn', axis=1, tiled=True)  36 us
    reduce_scatter x1, waiting for transfers between devices, per_device(): lax.psum_scatter(slot_partial.astype(jnp.bfloat16), 'ffn', scatter_dimens...  30.9 us
    reshape x2, local copies, waits for them, and re-layouts, pack(): return packed.reshape(groups, capacity, rows.shape[1])  14.6 us
  transfers between devices with their start and end apart: 12, of which 8 were waited for; matrix products, arithmetic and copies ran while one was open for 16% of the time, Pallas kernels for 0%

profile of v1, /device:TPU:1, one launch (start us, length us, event | category | flops | bytes accessed | tf_op | source)
XLA Modules:
  0.0 571.0 jit_solution(7887270232983557613)
XLA Ops:
  17.7 5.0 all-to-all-start
  24.3 36.0 %all-gather.7.cloned.1.call-done = bf16[128,7168]{1,0:T(8,128)(2,1)} async-done(((bf16[128,1792]{1,0:T(8,128)(2,1)}), bf16[128,7168]{1,0:T(8,128)(2,1)}) %all-gather.7.cloned.1.call-update) | async-done | bytes 1835024 | tf_op jit(solution)/shard_map/all_gather | solution.py:39
  60.3 4.9 convolution_convert_fusion
  65.2 7.3 %reshape.113 = bf16[16,20,7168]{2,1,0:T(8,128)(2,1)} reshape(bf16[320,7168]{1,0:T(8,128)(2,1)} %convolution_convert_fusion) | data formatting | bytes 9175040 | tf_op jit(solution)/shard_map/reshape | solution.py:36
  72.5 6.3 %all-to-all-done = bf16[4,256,1792]{1,2,0:T(8,128)(2,1)} async-done(((bf16[4,256,1792]{1,2,0:T(8,128)(2,1)}), bf16[4,256,1792]{1,2,0:T(8,128)(2,1)}, u32[]{:S(2)}, u32[]{:S(2)}) %all-to-all-start) | async-done | bytes 3670048 | tf_op jit(solution)/shard_map/all_to_all | solution.py:41
  78.8 12.0 %all-to-all-start.2 = ((bf16[16,20,7168]{2,1,0:T(8,128)(2,1)}), bf16[16,20,7168]{2,1,0:T(8,128)(2,1)}, u32[]{:S(2)}, u32[]{:S(2)}) async-start(bf16[16,20,7168]{2,1,0:T(8,128)(2,1)} %reshape.113), calls=%async_computation.2 | async-start | bytes 11010048 | tf_op jit(solution)/shard_map/all_to_all | solution.py:51
  92.0 5.5 convolution_convert_fusion.1
  97.5 7.3 %reshape.111 = bf16[16,20,7168]{2,1,0:T(8,128)(2,1)} reshape(bf16[320,7168]{1,0:T(8,128)(2,1)} %convolution_convert_fusion.1) | data formatting | bytes 9175040 | tf_op jit(solution)/shard_map/reshape | solution.py:36
  104.8 107.6 %all-to-all-done.2 = bf16[16,20,7168]{2,1,0:T(8,128)(2,1)} async-done(((bf16[16,20,7168]{2,1,0:T(8,128)(2,1)}), bf16[16,20,7168]{2,1,0:T(8,128)(2,1)}, u32[]{:S(2)}, u32[]{:S(2)}) %all-to-all-start.2) | async-done | bytes 4587552 | tf_op jit(solution)/shard_map/all_to_all | solution.py:51
  212.4 5.5 all-to-all-start.1
  218.7 7.3 %reshape.114 = bf16[320,7168]{1,0:T(8,128)(2,1)} reshape(bf16[16,20,7168]{2,1,0:T(8,128)(2,1)} %all-to-all-done.2) | data formatting | bytes 9175040 | tf_op jit(solution)/shard_map/reshape | solution.py:58
  226.1 113.5 %all-to-all-done.1 = bf16[16,20,7168]{2,1,0:T(8,128)(2,1)} async-done(((bf16[16,20,7168]{2,1,0:T(8,128)(2,1)}), bf16[16,20,7168]{2,1,0:T(8,128)(2,1)}, u32[]{:S(2)}, u32[]{:S(2)}) %all-to-all-start.1) | async-done | bytes 4587552 | tf_op jit(solution)/shard_map/all_to_all | solution.py:54
  339.5 7.3 %reshape.112 = bf16[320,7168]{1,0:T(8,128)(2,1)} reshape(bf16[16,20,7168]{2,1,0:T(8,128)(2,1)} %all-to-all-done.1) | data formatting | bytes 9175040 | tf_op jit(solution)/shard_map/reshape | solution.py:59
  346.9 4.8 fusion.6
  351.7 4.8 fusion.9
  356.5 5.0 multiply_convert_fusion.2
  367.2 6.3 %fusion.3 = bf16[1,256,7168]{2,1,0:T(8,128)(2,1)} fusion(bf16[320,7168]{1,0:T(8,128)(2,1)} %reshape.112, f32[320,256]{1,0:T(8,128)S(1)} %fusion.9, f32[320,256]{1,0:T(8,128)S(1)} %fusion.6), kind=kOutput, calls=%fused_computation.9 | convolution fusion | flops 1176731648 | bytes 8912896 | tf_op jit(solution)/shard_map/dot_general | solution.py:78
  373.5 6.3 %fusion.2 = bf16[1,7168,256]{2,1,0:T(8,128)(2,1)} fusion(bf16[320,7168]{1,0:T(8,128)(2,1)} %reshape.114, bf16[320,256]{1,0:T(8,128)(2,1)S(1)} %get-tuple-element.4), kind=kOutput, calls=%fused_computation.8 | convolution fusion | flops 1176240128 | bytes 8421376 | tf_op jit(solution)/shard_map/dot_general | solution.py:77
  380.1 6.3 %fusion.1 = bf16[1,7168,256]{2,1,0:T(8,128)(2,1)} fusion(bf16[320,7168]{1,0:T(8,128)(2,1)} %reshape.114, bf16[320,256]{1,0:T(8,128)(2,1)S(1)} %get-tuple-element.5), kind=kOutput, calls=%fused_computation.7 | convolution fusion | flops 1176240128 | bytes 8421376 | tf_op jit(solution)/shard_map/dot_general | solution.py:74
  386.4 30.9 %reduce-scatter.5.cloned.1.call-done = bf16[320,1792]{1,0:T(8,128)(2,1)} async-done(((bf16[320,7168]{1,0:T(8,128)(2,1)}), bf16[320,1792]{1,0:T(8,128)(2,1)}) %reduce-scatter.5.cloned.1.call-update) | async-done | bytes 1146896 | tf_op jit(solution)/shard_map/reduce_scatter | solution.py:96
  419.6 7.8 %all-to-all-start.3 = ((bf16[16,20,1792]{2,1,0:T(8,128)(2,1)}), bf16[16,20,1792]{2,1,0:T(8,128)(2,1)S(1)}, u32[]{:S(2)}, u32[]{:S(2)}) async-start(bf16[16,20,1792]{2,1,0:T(8,128)(2,1)} %reshape.115), calls=%async_computation.4 | async-start | bytes 2752512 | tf_op jit(solution)/shard_map/all_to_all | solution.py:100
  427.6 37.2 %reduce-scatter.11.cloned.1.call-done = bf16[1,256,1792]{2,1,0:T(8,128)(2,1)} async-done(((bf16[1,256,7168]{2,1,0:T(8,128)(2,1)}), bf16[1,256,1792]{2,1,0:T(8,128)(2,1)}) %reduce-scatter.11.cloned.1.call-update) | async-done | bytes 917520 | tf_op jit(solution)/shard_map/reduce_scatter | solution.py:86
  467.3 44.8 %reduce-scatter.9.cloned.1.call-done = bf16[1,1792,256]{2,1,0:T(8,128)(2,1)} async-done(((bf16[1,7168,256]{2,1,0:T(8,128)(2,1)}), bf16[1,1792,256]{2,1,0:T(8,128)(2,1)}) %reduce-scatter.9.cloned.1.call-update) | async-done | bytes 917520 | tf_op jit(solution)/shard_map/reduce_scatter | solution.py:83
  514.7 44.8 %reduce-scatter.7.cloned.1.call-done = bf16[1,1792,256]{2,1,0:T(8,128)(2,1)} async-done(((bf16[1,7168,256]{2,1,0:T(8,128)(2,1)}), bf16[1,1792,256]{2,1,0:T(8,128)(2,1)}) %reduce-scatter.7.cloned.1.call-update) | async-done | bytes 917520 | tf_op jit(solution)/shard_map/reduce_scatter | solution.py:80
  (57 shorter events, 31.1 us)
Async XLA Ops:
  8.0 52.3 %all-gather.7.cloned.1.call-start = ((), (), s32[]{:S(2)}) async-start(), calls=%async_computation.9 | async-start | bytes 2293760 | tf_op jit(solution)/shard_map/all_gather | solution.py:39
  17.7 5.0 copy-start.2
  17.7 61.1 %all-to-all-start = ((bf16[4,256,1792]{1,2,0:T(8,128)(2,1)}), bf16[4,256,1792]{1,2,0:T(8,128)(2,1)}, u32[]{:S(2)}, u32[]{:S(2)}) async-start(bf16[4,256,1792]{1,2,0:T(8,128)(2,1)} %stack.3), calls=%async_computation | async-start | bytes 7340032 | tf_op jit(solution)/shard_map/all_to_all | solution.py:41
  78.8 133.6 %all-to-all-start.2 = ((bf16[16,20,7168]{2,1,0:T(8,128)(2,1)}), bf16[16,20,7168]{2,1,0:T(8,128)(2,1)}, u32[]{:S(2)}, u32[]{:S(2)}) async-start(bf16[16,20,7168]{2,1,0:T(8,128)(2,1)} %reshape.113), calls=%async_computation.2 | async-start | bytes 11010048 | tf_op jit(solution)/shard_map/all_to_all | solution.py:51
  90.8 256.1 %all-gather.11.cloned.1.call-start = ((), (), s32[]{:S(2)}) async-start(), calls=%async_computation.11 | async-start | bytes 4587520 | tf_op jit(solution)/shard_map/all_gather | solution.py:63
  91.4 260.3 %all-gather.9.cloned.1.call-start = ((), (), s32[]{:S(2)}) async-start(), calls=%async_computation.10 | async-start | bytes 4587520 | tf_op jit(solution)/shard_map/all_gather | solution.py:64
  212.4 127.1 %all-to-all-start.1 = ((bf16[16,20,7168]{2,1,0:T(8,128)(2,1)}), bf16[16,20,7168]{2,1,0:T(8,128)(2,1)}, u32[]{:S(2)}, u32[]{:S(2)}) async-start(bf16[16,20,7168]{2,1,0:T(8,128)(2,1)} %reshape.111), calls=%async_computation.1 | async-start | bytes 11010048 | tf_op jit(solution)/shard_map/all_to_all | solution.py:54
  217.9 138.6 %all-gather.5.cloned.1.call-start = ((), (), s32[]{:S(2)}) async-start(), calls=%async_computation.8 | async-start | bytes 4587520 | tf_op jit(solution)/shard_map/all_gather | solution.py:65
  218.5 198.8 %reduce-scatter.5.cloned.1.call-start = ((), (), s32[]{:S(2)}) async-start(), calls=%async_computation.12 | async-start | bytes 5734400 | tf_op jit(solution)/shard_map/reduce_scatter | solution.py:96
  356.5 5.0 copy-start
  361.5 2.0 copy-start.1
  367.1 97.6 %reduce-scatter.11.cloned.1.call-start = ((), (), s32[]{:S(2)}) async-start(), calls=%async_computation.15 | async-start | bytes 4587520 | tf_op jit(solution)/shard_map/reduce_scatter | solution.py:86
  373.5 138.6 %reduce-scatter.9.cloned.1.call-start = ((), (), s32[]{:S(2)}) async-start(), calls=%async_computation.14 | async-start | bytes 4587520 | tf_op jit(solution)/shard_map/reduce_scatter | solution.py:83
  379.8 179.6 %reduce-scatter.7.cloned.1.call-start = ((), (), s32[]{:S(2)}) async-start(), calls=%async_computation.13 | async-start | bytes 4587520 | tf_op jit(solution)/shard_map/reduce_scatter | solution.py:80
  419.6 142.4 %all-to-all-start.3 = ((bf16[16,20,1792]{2,1,0:T(8,128)(2,1)}), bf16[16,20,1792]{2,1,0:T(8,128)(2,1)S(1)}, u32[]{:S(2)}, u32[]{:S(2)}) async-start(bf16[16,20,1792]{2,1,0:T(8,128)(2,1)} %reshape.115), calls=%async_computation.4 | async-start | bytes 2752512 | tf_op jit(solution)/shard_map/all_to_all | solution.py:100
Sparse Core Ops, SparseCore 0:
  10.6 49.6 all-gather.6
  367.3 49.9 reduce-scatter.4
  419.8 44.8 reduce-scatter.10
  467.2 44.8 reduce-scatter.8
  514.5 44.8 reduce-scatter.6
Sparse Core Ops, SparseCore 1:
  93.1 45.2 all-gather.10
  140.1 46.5 all-gather.8
  220.2 45.2 all-gather.4
